TPU v7x, 32 devices: a whole 2x2x4 slice. The times are simulated.
32 devices in a mesh: term: 2 (over x), sector: 16 (over z, y, core).
Axes of the slice: x: 2, y: 2, z: 4, core: 2. Of those that a mesh axis runs over, the one named last changes fastest.
Arguments:
- psi_start: bfloat16 [128, 256, 256], P('sector'), may hold values from -6 to 6
- left_env: bfloat16 [6, 128, 256, 256], P('term', 'sector')
- right_env: bfloat16 [6, 128, 256, 256], P('term', 'sector')
- connect: int32 [6, 128], P('term', 'sector'), may hold values from 0 to 127, as said below
- sector_dims: int32 [2, 128], P(None, 'sector'), may hold values from 64 to 256
- precond: bfloat16 [128, 256, 256], P('sector'), may hold values from 0.5 to 4
Outputs:
- projected: float32 [3, 3], replicated
- last_vector: float32 [128, 256, 256], P('sector', 'term')
- new_env: bfloat16 [6, 128, 256, 256], P('term', 'sector')
Inputs may be any that keep to these rules, and one draw needn't show every extreme that they name: connect[t, s] differs from s by at most 8.
All inputs are finite; a program needn't handle non-finite values.
Results may differ from a plain program's by a relative error of at most 0.012.
Values may be sent and summed in bfloat16 or wider, within the bound.
A program may use at most 128 MiB of HBM per device.

v0:
```python
import jax
import jax.numpy as jnp
from jax import lax
from jax.sharding import PartitionSpec as P

epsilon = 1e-06


def with_halo(block, sides, width):
    for axis, dim in sides:
        count = lax.axis_size(axis)
        forward = [(i, i + 1) for i in range(count - 1)]
        backward = [(target, source) for source, target in forward]
        low = lax.ppermute(
            lax.slice_in_dim(block, block.shape[dim] - width, None, axis=dim), axis, forward
        )
        high = lax.ppermute(lax.slice_in_dim(block, 0, width, axis=dim), axis, backward)
        block = jnp.concatenate([low, block, high], axis=dim)
    return block


def on_device(psi_start, left_env, right_env, connect, sector_dims, precond):
    blocks = psi_start.shape[0]
    width = psi_start.shape[1]
    devices = lax.axis_size("sector")
    pieces = lax.axis_size("term")
    terms_here = left_env.shape[0]
    entries = float(blocks * devices * width * width)
    local_source = connect - (lax.axis_index("sector") * blocks - blocks)
    share = width // pieces
    share_start = lax.axis_index("term") * share
    row_ids = lax.broadcasted_iota(jnp.int32, (blocks, width, width), 1)
    col_ids = lax.broadcasted_iota(jnp.int32, (blocks, width, width), 2)
    keep = (row_ids < sector_dims[0][:, None, None]) & (col_ids < sector_dims[1][:, None, None])
    mask = keep.astype(jnp.float32)
    start_rows = psi_start.astype(jnp.float32) * mask
    divisor = precond.astype(jnp.float32)

    def totals(values):
        stacked = jnp.stack(values)
        summed = lax.psum(stacked, "sector")
        return summed / entries

    norm_start = totals([jnp.sum(start_rows * start_rows)])[0]
    basis = [start_rows / jnp.sqrt(norm_start + epsilon)]
    sigmas = []
    env_list = []
    for which in range(3):
        vector_b = basis[which].astype(jnp.bfloat16)
        extended = with_halo(vector_b, (("sector", 0),), blocks)
        with_env = which == 2
        total = jnp.zeros((blocks, width, width), jnp.float32)
        own_blocks = extended[blocks : 2 * blocks]
        envs = []
        for apply_which in range(terms_here):
            source = jnp.take(extended, local_source[apply_which], axis=0)
            half = jnp.einsum(
                "sij,sjk->sik", left_env[apply_which], source, preferred_element_type=jnp.float32
            ).astype(jnp.bfloat16)
            total = total + jnp.einsum(
                "sik,slk->sil", half, right_env[apply_which], preferred_element_type=jnp.float32
            )
            if with_env:
                env_one = jnp.einsum(
                    "sji,sjk->sik", own_blocks, half, preferred_element_type=jnp.float32
                ) * width ** (-0.5)
                envs.append(env_one.astype(jnp.bfloat16))
        sigma = lax.psum(total, "term")
        sigma, env_list = (sigma * mask, envs)
        sigmas.append(sigma)
        if which < 2:
            theta = totals([jnp.sum(basis[which] * sigma)])[0]
            corr = (sigma - theta * basis[which]) / divisor
            correlations = totals([jnp.sum(member * corr) for member in basis])
            for position in range(len(basis)):
                corr = corr - correlations[position] * basis[position]
            length = totals([jnp.sum(corr * corr)])[0]
            basis.append(corr / jnp.sqrt(length + epsilon))
    products = totals([jnp.sum(basis[row] * sigmas[col]) for row in range(3) for col in range(3)])
    projected = products.reshape(3, 3)
    last_vector = lax.dynamic_slice_in_dim(basis[2], share_start, share, 1)
    return (projected, last_vector, jnp.stack(env_list))


def solution(mesh):
    placed = (
        P("sector", None, None),
        P("term", "sector", None, None),
        P("term", "sector", None, None),
        P("term", "sector"),
        P(None, "sector"),
        P("sector", None, None),
    )
    return jax.shard_map(
        on_device,
        mesh=mesh,
        in_specs=placed,
        out_specs=(P(), P("sector", "term", None), P("term", "sector", None, None)),
        check_vma=False,
    )
```

profile of v0, /device:TPU:0, one launch (start us, length us, event | category | flops | bytes accessed | tf_op | source)
XLA Modules:
  0.0 646.5 jit_solution(17308843335064194327)
XLA Ops:
  7.2 0.8 slice_bitcast_fusion.1
  8.0 2.4 multiply_reduce_fusion.14
  10.4 35.6 %psum.77 = f32[1]{0:T(128)} all-reduce(f32[1]{0:T(128)} %bitcast.2), channel_id=1, replica_groups=mesh['term'=2,'sector'=16] {'sector'}, use_global_device_ids=true, to_apply=%region_1.0 | all-reduce | flops 1 | bytes 8 | tf_op jit(solution)/shard_map/psum | solution.py:41
  46.7 1.8 fusion.119
  48.5 1.4 collective-permute-start
  49.9 1.3 collective-permute-start.1
  51.2 0.8 collective-permute-done
  52.1 1.0 copy-done.15
  53.0 1.5 collective-permute-done.1
  54.5 2.0 pad_maximum_fusion
  56.6 1.6 gather_fusion.1
  58.2 1.6 gather_fusion
  59.7 1.6 gather_fusion.2
  61.3 4.2 fusion.3
  65.5 3.7 fusion.2
  69.2 5.0 add_add_fusion.2
  74.3 79.1 %all-reduce.4.cloned.1.call-done = f32[8,256,256]{2,1,0:T(8,128)} async-done(((f32[8,256,256]{2,1,0:T(8,128)}), f32[8,256,256]{2,1,0:T(8,128)}) %all-reduce.4.cloned.1.call-update) | async-done | bytes 2097168 | tf_op jit(solution)/shard_map/psum | solution.py:68
  153.4 3.0 multiply_reduce_fusion.13
  156.5 33.6 %psum.79 = f32[1]{0:T(128)} all-reduce(f32[1]{0:T(128)} %bitcast.13), channel_id=1, replica_groups=mesh['term'=2,'sector'=16] {'sector'}, use_global_device_ids=true, to_apply=%region_4.6 | all-reduce | flops 1 | bytes 8 | tf_op jit(solution)/shard_map/psum | solution.py:41
  190.8 2.8 multiply_reduce_fusion.12
  193.6 30.1 %psum.80 = f32[1]{0:T(128)} all-reduce(f32[1]{0:T(128)} %bitcast.15), channel_id=1, replica_groups=mesh['term'=2,'sector'=16] {'sector'}, use_global_device_ids=true, to_apply=%region_6.8 | all-reduce | flops 1 | bytes 8 | tf_op jit(solution)/shard_map/psum | solution.py:41
  224.3 3.6 multiply_reduce_fusion.11
  227.9 30.1 %psum.81 = f32[1]{0:T(128)} all-reduce(f32[1]{0:T(128)} %bitcast.17), channel_id=1, replica_groups=mesh['term'=2,'sector'=16] {'sector'}, use_global_device_ids=true, to_apply=%region_8.10 | all-reduce | flops 1 | bytes 8 | tf_op jit(solution)/shard_map/psum | solution.py:41
  258.9 1.8 collective-permute-start.2
  260.8 1.3 collective-permute-start.3
  262.1 0.9 collective-permute-done.2
  263.0 2.4 collective-permute-done.3
  265.3 1.8 pad_maximum_fusion.1
  267.2 3.5 gather_fusion.4
  270.6 3.5 gather_fusion.3
  274.1 3.5 gather_fusion.5
  277.6 4.0 fusion.5
  281.6 4.0 fusion.4
  285.6 5.3 add_add_fusion.1
  291.2 79.4 %all-reduce.6.cloned.1.call-done = f32[8,256,256]{2,1,0:T(8,128)} async-done(((f32[8,256,256]{2,1,0:T(8,128)}), f32[8,256,256]{2,1,0:T(8,128)}) %all-reduce.6.cloned.1.call-update) | async-done | bytes 2097168 | tf_op jit(solution)/shard_map/psum | solution.py:68
  370.5 2.9 multiply_reduce_fusion.9
  373.4 33.6 %psum.83 = f32[1]{0:T(128)} all-reduce(f32[1]{0:T(128)} %bitcast.20), channel_id=1, replica_groups=mesh['term'=2,'sector'=16] {'sector'}, use_global_device_ids=true, to_apply=%region_12.14 | all-reduce | flops 1 | bytes 8 | tf_op jit(solution)/shard_map/psum | solution.py:41
  407.7 3.9 multiply_reduce_fusion.8
  411.6 1.3 pad_maximum_fusion.4
  413.0 29.5 %psum.84 = f32[2]{0:T(128)S(1)} all-reduce(f32[2]{0:T(128)S(1)} %pad_maximum_fusion.4), channel_id=1, replica_groups=mesh['term'=2,'sector'=16] {'sector'}, use_global_device_ids=true, to_apply=%region_15.17 | all-reduce | flops 2 | bytes 16 | tf_op jit(solution)/shard_map/psum | solution.py:41
  443.1 6.4 multiply_reduce_fusion.6
  449.5 30.1 %psum.85 = f32[1]{0:T(128)} all-reduce(f32[1]{0:T(128)} %bitcast.26), channel_id=1, replica_groups=mesh['term'=2,'sector'=16] {'sector'}, use_global_device_ids=true, to_apply=%region_17.19 | all-reduce | flops 1 | bytes 8 | tf_op jit(solution)/shard_map/psum | solution.py:41
  480.3 3.2 fusion.121
  483.5 1.8 collective-permute-start.4
  485.3 1.3 collective-permute-start.5
  486.6 0.9 collective-permute-done.4
  487.5 2.4 collective-permute-done.5
  489.9 1.8 pad_maximum_fusion.2
  491.7 3.5 gather_fusion.6
  495.2 3.5 gather_fusion.7
  498.7 3.5 gather_fusion.8
  502.2 2.3 convolution_convert_fusion.8
  504.7 2.2 convolution_convert_fusion.7
  507.5 1.7 copy-done.5
  510.2 1.9 add_add_fusion
  512.2 2.4 constant_dynamic-slice_fusion
  514.6 1.6 fusion.6
  516.2 1.5 fusion.7
  517.7 1.5 fusion.8
  519.2 72.6 %all-reduce.8.cloned.1.call-done = f32[8,256,256]{2,1,0:T(8,128)} async-done(((f32[8,256,256]{2,1,0:T(8,128)}), f32[8,256,256]{2,1,0:T(8,128)}) %all-reduce.8.cloned.1.call-update) | async-done | bytes 2097168 | tf_op jit(solution)/shard_map/psum | solution.py:68
  591.7 4.9 multiply_reduce_fusion
  596.6 5.8 stack.81
  602.4 3.9 pad_maximum_fusion.3
  606.3 33.0 %psum.87 = f32[9]{0:T(128)S(1)} all-reduce(f32[9]{0:T(128)S(1)} %stack.81), channel_id=1, replica_groups=mesh['term'=2,'sector'=16] {'sector'}, use_global_device_ids=true, to_apply=%region_25.27 | all-reduce | flops 9 | bytes 72 | tf_op jit(solution)/shard_map/psum | solution.py:41
  (50 shorter events, 3.7 us)
Async XLA Ops:
  7.2 44.0 %copy-start.16 = (s32[3,8]{1,0:T(4,128)S(1)}, s32[3,8]{1,0:T(4,128)}, u32[]{:S(2)}) copy-start(s32[3,8]{1,0:T(4,128)} %param.11) | copy-start | bytes 292
  7.2 146.2 %all-reduce.4.cloned.1.call-start = ((), (), s32[]{:S(2)}) async-start(), calls=%async_computation | async-start | bytes 4194304 | tf_op jit(solution)/shard_map/psum | solution.py:68
  48.5 3.6 copy-start.10
  48.5 3.6 collective-permute-start
  49.9 4.7 collective-permute-start.1
  52.1 1.0 copy-start.15
  61.3 4.2 copy-start.4
  74.2 79.2 %copy-start = (bf16[8,256,256]{2,1,0:T(8,128)(2,1)S(1)}, bf16[8,256,256]{2,1,0:T(8,128)(2,1)}, u32[]{:S(2)}) copy-start(bf16[8,256,256]{2,1,0:T(8,128)(2,1)} %param.8) | copy-start | bytes 3145732
  74.2 296.3 %all-reduce.6.cloned.1.call-start = ((), (), s32[]{:S(2)}) async-start(), calls=%async_computation.1 | async-start | bytes 4194304 | tf_op jit(solution)/shard_map/psum | solution.py:68
  153.4 37.3 %copy-start.1 = (f32[8,256,256]{2,1,0:T(8,128)S(1)}, f32[8,256,256]{2,1,0:T(8,128)}, u32[]{:S(2)}) copy-start(f32[8,256,256]{2,1,0:T(8,128)} %all-reduce.4.cloned.1.call-done) | copy-start | bytes 6291460
  258.9 4.0 collective-permute-start.2
  260.8 4.6 collective-permute-start.3
  290.9 300.8 %all-reduce.8.cloned.1.call-start = ((), (), s32[]{:S(2)}) async-start(), calls=%async_computation.2 | async-start | bytes 4194304 | tf_op jit(solution)/shard_map/psum | solution.py:68
  483.5 6.4 copy-start.2
  483.5 4.0 collective-permute-start.4
  485.3 4.6 collective-permute-start.5
  502.2 2.5 copy-start.13
  504.7 5.0 copy-start.6
  504.7 2.2 copy-start.14
  506.9 2.8 copy-start.8
  506.9 2.3 copy-start.5
  509.2 1.0 copy-start.11
  512.1 2.4 copy-start.3
  512.2 2.4 copy-start.7
  514.6 1.6 copy-start.9
  516.2 1.5 copy-start.12
Sparse Core Ops, SparseCore 0:
  74.4 79.0 all-reduce.3
  291.0 79.4 all-reduce.5
  512.3 79.4 all-reduce.7
where the time goes:
time: 648 us; the launch traced here: 646 us
  blocking collectives  256 us (40%)
  waiting for transfers between devices  240 us (37%)
  other arithmetic  46.1 us (7%)
  local copies, waits for them, and re-layouts  38.9 us (6%)
  matrix products  38.6 us (6%)
  between operations  18 us (3%)
  starting transfers between devices  9.19 us (1%)
    psum x8, blocking collectives, totals(): summed = lax.psum(stacked, 'sector')  256 us
    psum x3, waiting for transfers between devices, on_device(): sigma = lax.psum(total, 'term')  231 us
    dot_general x9, matrix products, on_device(): jnp.einsum('sik,slk->sil', half, right_env[apply_which], preferred_elemen...  29 us
    gather x9, local copies, waits for them, and re-layouts, on_device(): source = jnp.take(extended, local_source[apply_which], axis=0)  25.7 us
  transfers between devices with their start and end apart: 9, of which 9 were waited for; matrix products, arithmetic and copies ran while one was open for 1% of the time, Pallas kernels for 0%

commit v1 on v0

--- a/solution.py
+++ b/solution.py
@@ -4,6 +4,12 @@
 from jax.sharding import PartitionSpec as P
 
 epsilon = 1e-06
+
+
+def gather_and_add(x, axis):
+    pieces = lax.all_gather(x, axis, axis=0, tiled=False)
+    total = pieces.sum(axis=0)
+    return total
 
 
 def with_halo(block, sides, width):
@@ -38,7 +44,7 @@
 
     def totals(values):
         stacked = jnp.stack(values)
-        summed = lax.psum(stacked, "sector")
+        summed = gather_and_add(stacked, "sector")
         return summed / entries
 
     norm_start = totals([jnp.sum(start_rows * start_rows)])[0]

time: 648 us -> 656 us (1.012)
  local copies, waits for them, and re-layouts: 38.9 us -> 53.1 us
    psum x8 -> x0, blocking collectives: 256 us -> none  [totals(): summed = lax.psum(stacked, 'sector')]
    unnamed x0 -> x8, blocking collectives: none -> 252 us
    unnamed x34 -> x44, local copies, waits for them, and re-layouts: 2.96 us -> 12.7 us
where the time goes in v1:
time: 656 us; the launch traced here: 654 us
  blocking collectives  252 us (38%)
  waiting for transfers between devices  239 us (36%)
  local copies, waits for them, and re-layouts  53.1 us (8%)
  other arithmetic  47.7 us (7%)
  matrix products  34 us (5%)
  between operations  19.2 us (3%)
  starting transfers between devices  9.41 us (1%)
    unnamed x8, blocking collectives  252 us
    psum x3, waiting for transfers between devices, on_device(): sigma = lax.psum(total, 'term')  229 us
    gather x9, local copies, waits for them, and re-layouts, on_device(): source = jnp.take(extended, local_source[apply_which], axis=0)  30.4 us
    dot_general x9, matrix products, on_device(): jnp.einsum('sik,slk->sil', half, right_env[apply_which], preferred_elemen...  27.5 us
  transfers between devices with their start and end apart: 9, of which 9 were waited for; matrix products, arithmetic and copies ran while one was open for 1% of the time, Pallas kernels for 0%

profile of v1, /device:TPU:0, one launch (start us, length us, event | category | flops | bytes accessed | tf_op | source)
XLA Modules:
  0.0 654.1 jit_solution(16749817365554523841)
XLA Ops:
  8.0 1.2 dynamic-slice
  9.2 2.4 multiply_reduce_fusion.14
  11.7 1.3 dynamic-update-slice
  13.0 34.9 %all-reduce = f32[16]{0:T(128)S(1)} all-reduce(f32[16]{0:T(128)S(1)} %dynamic-update-slice), channel_id=1, replica_groups=mesh['term'=2,'sector'=16] {'sector'}, use_global_device_ids=true, to_apply=%add | all-reduce | flops 16 | bytes 128
  49.2 1.8 fusion.119
  51.0 1.4 collective-permute-start
  52.4 1.3 collective-permute-start.1
  53.8 0.8 collective-permute-done
  54.6 2.4 collective-permute-done.1
  56.9 1.8 pad_maximum_fusion
  58.8 3.5 gather_fusion.1
  62.3 3.5 gather_fusion
  65.7 2.5 gather_fusion.2
  68.2 2.7 fusion.3
  70.9 4.0 fusion.2
  75.0 4.4 add_add_fusion.2
  79.5 78.3 %all-reduce.12.cloned.1.call-done = f32[8,256,256]{2,1,0:T(8,128)} async-done(((f32[8,256,256]{2,1,0:T(8,128)}), f32[8,256,256]{2,1,0:T(8,128)}) %all-reduce.12.cloned.1.call-update) | async-done | bytes 2097168 | tf_op jit(solution)/shard_map/psum | solution.py:74
  157.7 3.0 multiply_reduce_fusion.13
  160.8 1.3 dynamic-update-slice.1
  162.1 33.0 %all-reduce.1 = f32[16]{0:T(128)S(1)} all-reduce(f32[16]{0:T(128)S(1)} %dynamic-update-slice.1), channel_id=1, replica_groups=mesh['term'=2,'sector'=16] {'sector'}, use_global_device_ids=true, to_apply=%add.1 | all-reduce | flops 16 | bytes 128
  196.3 2.8 multiply_reduce_fusion.12
  199.1 1.3 dynamic-update-slice.2
  200.5 29.5 %all-reduce.2 = f32[16]{0:T(128)S(1)} all-reduce(f32[16]{0:T(128)S(1)} %dynamic-update-slice.2), channel_id=1, replica_groups=mesh['term'=2,'sector'=16] {'sector'}, use_global_device_ids=true, to_apply=%add.2 | all-reduce | flops 16 | bytes 128
  231.2 3.6 multiply_reduce_fusion.11
  234.8 1.3 dynamic-update-slice.3
  236.1 29.5 %all-reduce.3 = f32[16]{0:T(128)S(1)} all-reduce(f32[16]{0:T(128)S(1)} %dynamic-update-slice.3), channel_id=1, replica_groups=mesh['term'=2,'sector'=16] {'sector'}, use_global_device_ids=true, to_apply=%add.3 | all-reduce | flops 16 | bytes 128
  267.1 1.8 collective-permute-start.2
  268.9 1.5 collective-permute-start.3
  271.1 2.4 collective-permute-done.3
  273.5 1.8 pad_maximum_fusion.1
  275.3 3.5 gather_fusion.4
  278.8 3.5 gather_fusion.3
  282.3 3.5 gather_fusion.5
  285.8 4.0 fusion.5
  289.8 4.0 fusion.4
  293.8 5.4 add_add_fusion.1
  299.2 79.6 %all-reduce.14.cloned.1.call-done = f32[8,256,256]{2,1,0:T(8,128)} async-done(((f32[8,256,256]{2,1,0:T(8,128)}), f32[8,256,256]{2,1,0:T(8,128)}) %all-reduce.14.cloned.1.call-update) | async-done | bytes 2097168 | tf_op jit(solution)/shard_map/psum | solution.py:74
  378.8 2.8 multiply_reduce_fusion.9
  381.6 1.2 dynamic-update-slice.4
  383.4 33.0 %all-reduce.4 = f32[16]{0:T(128)S(1)} all-reduce(f32[16]{0:T(128)S(1)} %dynamic-update-slice.4), channel_id=1, replica_groups=mesh['term'=2,'sector'=16] {'sector'}, use_global_device_ids=true, to_apply=%add.4 | all-reduce | flops 16 | bytes 128
  417.7 3.8 multiply_reduce_fusion.8
  421.5 1.5 maximum_dynamic-update-slice_fusion
  423.0 29.5 %all-reduce.5 = f32[32]{0:T(128)S(1)} all-reduce(f32[32]{0:T(128)S(1)} %maximum_dynamic-update-slice_fusion), channel_id=2, replica_groups=mesh['term'=2,'sector'=16] {'sector'}, use_global_device_ids=true, to_apply=%add.5 | all-reduce | flops 32 | bytes 256
  453.2 6.4 multiply_reduce_fusion.6
  459.6 1.3 dynamic-update-slice.6
  460.9 29.5 %all-reduce.6 = f32[16]{0:T(128)S(1)} all-reduce(f32[16]{0:T(128)S(1)} %dynamic-update-slice.6), channel_id=1, replica_groups=mesh['term'=2,'sector'=16] {'sector'}, use_global_device_ids=true, to_apply=%add.6 | all-reduce | flops 16 | bytes 128
  491.6 3.2 fusion.121
  494.8 1.8 collective-permute-start.4
  496.7 1.5 collective-permute-start.5
  498.9 2.4 collective-permute-done.5
  501.2 1.8 pad_maximum_fusion.2
  503.1 3.5 gather_fusion.6
  506.5 3.5 gather_fusion.7
  510.0 3.5 gather_fusion.8
  513.5 2.3 convolution_convert_fusion.2
  516.0 2.2 convolution_convert_fusion.1
  518.9 1.7 copy-done.4
  521.6 1.9 add_add_fusion
  524.2 2.4 constant_dynamic-slice_fusion
  529.6 2.0 pad_maximum_fusion.3
  531.6 71.6 %all-reduce.16.cloned.1.call-done = f32[8,256,256]{2,1,0:T(8,128)} async-done(((f32[8,256,256]{2,1,0:T(8,128)}), f32[8,256,256]{2,1,0:T(8,128)}) %all-reduce.16.cloned.1.call-update) | async-done | bytes 2097168 | tf_op jit(solution)/shard_map/psum | solution.py:74
  603.2 4.9 multiply_reduce_fusion
  608.1 5.5 stack.63
  613.8 33.0 %all-reduce.7 = f32[144]{0:T(256)S(1)} all-reduce(f32[144]{0:T(256)S(1)} %dynamic-update-slice.7), channel_id=3, replica_groups=mesh['term'=2,'sector'=16] {'sector'}, use_global_device_ids=true, to_apply=%add.7 | all-reduce | flops 144 | bytes 1152
  (70 shorter events, 12.7 us)
Async XLA Ops:
  7.2 46.5 %copy-start.13 = (s32[3,8]{1,0:T(4,128)S(1)}, s32[3,8]{1,0:T(4,128)}, u32[]{:S(2)}) copy-start(s32[3,8]{1,0:T(4,128)} %param.11) | copy-start | bytes 292
  7.2 150.6 %all-reduce.12.cloned.1.call-start = ((), (), s32[]{:S(2)}) async-start(), calls=%async_computation | async-start | bytes 4194304 | tf_op jit(solution)/shard_map/psum | solution.py:74
  51.0 3.6 collective-permute-start
  52.4 4.6 collective-permute-start.1
  79.4 78.4 %copy-start = (bf16[8,256,256]{2,1,0:T(8,128)(2,1)S(1)}, bf16[8,256,256]{2,1,0:T(8,128)(2,1)}, u32[]{:S(2)}) copy-start(bf16[8,256,256]{2,1,0:T(8,128)(2,1)} %param.8) | copy-start | bytes 3145732
  79.4 299.4 %all-reduce.14.cloned.1.call-start = ((), (), s32[]{:S(2)}) async-start(), calls=%async_computation.1 | async-start | bytes 4194304 | tf_op jit(solution)/shard_map/psum | solution.py:74
  157.7 38.6 %copy-start.1 = (f32[8,256,256]{2,1,0:T(8,128)S(1)}, f32[8,256,256]{2,1,0:T(8,128)}, u32[]{:S(2)}) copy-start(f32[8,256,256]{2,1,0:T(8,128)} %all-reduce.12.cloned.1.call-done) | copy-start | bytes 6291460
  267.1 4.0 collective-permute-start.2
  268.9 4.6 collective-permute-start.3
  299.2 304.0 %all-reduce.16.cloned.1.call-start = ((), (), s32[]{:S(2)}) async-start(), calls=%async_computation.2 | async-start | bytes 4194304 | tf_op jit(solution)/shard_map/psum | solution.py:74
  494.8 6.4 copy-start.2
  494.8 4.0 collective-permute-start.4
  496.7 4.6 collective-permute-start.5
  513.5 2.5 copy-start.11
  516.0 5.0 copy-start.5
  516.0 2.2 copy-start.12
  518.3 2.8 copy-start.7
  518.3 2.3 copy-start.4
  520.6 1.0 copy-start.9
  524.1 2.4 copy-start.3
  524.1 2.4 copy-start.6
  526.6 1.2 copy-start.8
  527.8 1.2 copy-start.10
Sparse Core Ops, SparseCore 0:
  79.5 78.1 all-reduce.11
  299.3 79.4 all-reduce.13
  523.7 79.4 all-reduce.15
